TPU v7x, 256 devices: a whole 4x4x8 slice. The times are simulated.
256 devices in a mesh: beam: 8 (over x, core), row: 32 (over y, z).
Axes of the slice: x: 4, y: 4, z: 8, core: 2. Of those that a mesh axis runs over, the one named last changes fastest.
Arguments:
- x_in: bfloat16 [4, 2, 16, 8192], P(None, None, None, 'beam'), may hold values from -6 to 6
- w_inner: bfloat16 [8192, 2, 16384], P('beam', None, 'row'), may hold values from -0.0625 to 0.0625
- w_bc: bfloat16 [8192, 2, 2048], P('beam', None, 'row'), may hold values from -0.0625 to 0.0625
- w_dt: bfloat16 [8192, 256], P('beam', 'row'), may hold values from -0.0625 to 0.0625
- conv_x_w: bfloat16 [4, 16384], P(None, 'row'), may hold values from -3 to 3
- conv_bc_w: bfloat16 [4, 2, 2048], P(None, None, 'row'), may hold values from -3 to 3
- dt_bias: float32 [256], P('row'), may hold values from -4 to 1
- a_log: float32 [256], P('row'), may hold values from 0 to 2.8
- d_skip: float32 [256], P('row'), may hold values from 0.5 to 2
- norm_gain: float32 [16384], P('row'), may hold values from 0.1 to 1.9
- w_out: bfloat16 [16384, 8192], P('row', 'beam'), may hold values from -0.046875 to 0.046875
- ssm_state: bfloat16 [2, 16, 256, 64, 256], P(None, 'beam', 'row'), may hold values from -6 to 6
- conv_x_state: bfloat16 [2, 16, 256, 64, 3], P(None, 'beam', 'row'), may hold values from -6 to 6
- conv_bc_state: bfloat16 [2, 16, 3, 2, 2048], P(None, 'beam', None, None, 'row'), may hold values from -6 to 6
- parents: int32 [4, 2, 16], replicated, may hold values from 0 to 15
Outputs:
- layer_out: bfloat16 [4, 32, 8192], P(None, 'row', 'beam')
- ssm_final: bfloat16 [2, 16, 256, 64, 256], P(None, 'beam', 'row')
- conv_x_final: bfloat16 [2, 16, 256, 64, 3], P(None, 'beam', 'row')
- conv_bc_final: bfloat16 [2, 16, 3, 2, 2048], P(None, 'beam', None, None, 'row')
All inputs are finite; a program needn't handle non-finite values.
Results may differ from a plain program's by a relative error of at most 0.0077.
Values may be sent and summed in bfloat16 or wider, within the bound.
No kernel may reach another device: no remote copies, remote signals or barrier semaphores. Data moves between devices by JAX's collectives and lax.ppermute only.
A program may use at most 64 MiB of HBM per device.

v0:
```python
import jax
import jax.numpy as jnp
from jax import lax
from jax.sharding import PartitionSpec as P

HEADS = 256
HDIM = 64
GROUPS = 8
EPS = 1e-05


def partner_2(shard, axis, stride):
    return lax.ppermute(shard, axis, [(i, i ^ 1 << stride) for i in range(lax.axis_size(axis))])


def stored(value):
    return lax.optimization_barrier(value.astype(jnp.bfloat16))


def local(
    x_in,
    w_inner,
    w_bc,
    w_dt,
    conv_x_w,
    conv_bc_w,
    dt_bias,
    a_log,
    d_skip,
    norm_gain,
    w_out,
    ssm_state,
    conv_x_state,
    conv_bc_state,
    parents,
):
    beam_index = lax.axis_index("beam")
    row_index = lax.axis_index("row")
    steps_all, sessions, width, d_local = x_in.shape
    local_beams = ssm_state.shape[1]
    heads_local = ssm_state.shape[2]
    head_dim = ssm_state.shape[3]
    tap_count = conv_x_w.shape[0]
    group_heads = HEADS // GROUPS
    group_index = row_index * heads_local // group_heads
    group_span = lax.axis_size("row") // GROUPS
    swap_rounds = group_span.bit_length() - 1
    w_inner4 = w_inner.reshape(d_local, 2, heads_local, head_dim)
    w_out3 = w_out.reshape(heads_local, head_dim, w_out.shape[1])
    conv_taps = conv_x_w.astype(jnp.float32).reshape(tap_count, heads_local, head_dim)
    gains = norm_gain.reshape(heads_local, head_dim)
    bc_taps = conv_bc_w.astype(jnp.float32)
    decay_rates = jnp.exp(a_log)
    group_mask = (jnp.arange(GROUPS, dtype=jnp.int32) == group_index).astype(jnp.float32)
    ssm_held = ssm_state
    conv_held = conv_x_state
    rim_held = conv_bc_state
    outputs = []
    for step in range(steps_all):
        parent = parents[step]
        own_parent = lax.dynamic_slice_in_dim(parent, beam_index * local_beams, local_beams, 1)
        pieces = (
            lax.all_gather(ssm_held, "beam", axis=1, tiled=True),
            lax.all_gather(conv_held, "beam", axis=1, tiled=True),
            lax.all_gather(rim_held, "beam", axis=1, tiled=True),
        )
        span_size = pieces[0].shape[1]
        beam_ids = jnp.arange(span_size, dtype=jnp.int32)
        choose = (own_parent[:, :, None] == beam_ids[None, None, :]).astype(jnp.bfloat16)
        ssm_held = jnp.einsum(
            "sij,sjhpn->sihpn", choose, pieces[0], preferred_element_type=jnp.float32
        ).astype(jnp.bfloat16)
        conv_held = jnp.einsum(
            "sij,sjhpk->sihpk", choose, pieces[1], preferred_element_type=jnp.float32
        ).astype(jnp.bfloat16)
        rim_held = jnp.einsum(
            "sij,sjkzc->sikzc", choose, pieces[2], preferred_element_type=jnp.float32
        ).astype(jnp.bfloat16)
        x_step = x_in[step]
        bc_part = jnp.einsum("sbd,dzk->sbzk", x_step, w_bc, preferred_element_type=jnp.float32)
        dt_part = jnp.einsum("sbd,dh->sbh", x_step, w_dt, preferred_element_type=jnp.float32)
        bc_sum, dt_sum = lax.psum((bc_part, dt_part), "beam")
        bc_new = stored(bc_sum)
        dt_raw = stored(dt_sum)
        bc_new = lax.dynamic_slice_in_dim(bc_new, beam_index * local_beams, local_beams, 1)
        dt_raw = lax.dynamic_slice_in_dim(dt_raw, beam_index * local_beams, local_beams, 1)
        inner_part = stored(
            lax.psum_scatter(
                jnp.einsum("sbd,dzhp->bszhp", x_step, w_inner4, preferred_element_type=jnp.float32),
                "beam",
                scatter_dimension=0,
                tiled=True,
            )
        )
        gate_in = jnp.transpose(inner_part[:, :, 0], (1, 0, 2, 3))
        x_new = jnp.transpose(inner_part[:, :, 1], (1, 0, 2, 3))
        mixed = jnp.sum(
            conv_held.astype(jnp.float32) * jnp.transpose(conv_taps[:-1], (1, 2, 0)), axis=-1
        )
        mixed = mixed + conv_taps[-1] * x_new.astype(jnp.float32)
        x_conv = stored(jax.nn.silu(mixed))
        conv_held = jnp.concatenate([conv_held[..., 1:], x_new[..., None]], axis=-1)
        mixed_bc = jnp.sum(rim_held.astype(jnp.float32) * bc_taps[:-1], axis=2) + bc_taps[
            -1
        ] * bc_new.astype(jnp.float32)
        bc_conv = stored(jax.nn.silu(mixed_bc))
        rim_held = jnp.concatenate([rim_held[:, :, 1:], bc_new[:, :, None]], axis=2)
        group_block = bc_conv
        for bit_number in range(swap_rounds):
            partner = partner_2(group_block, "row", bit_number)
            upper = jnp.bitwise_and(jnp.right_shift(row_index, bit_number), 1) == 1
            group_block = jnp.where(
                upper,
                jnp.concatenate([partner, group_block], axis=3),
                jnp.concatenate([group_block, partner], axis=3),
            )
        bc_group = group_block.astype(jnp.float32)
        b_in = bc_group[:, :, 0]
        c_out = bc_group[:, :, 1]
        step_size = jax.nn.softplus(dt_raw.astype(jnp.float32) + dt_bias)
        decay = jnp.exp(-decay_rates * step_size)
        x_val = x_conv.astype(jnp.float32)
        state = (
            decay[..., None, None] * ssm_held.astype(jnp.float32)
            + (step_size[..., None] * x_val)[..., None] * b_in[:, :, None, None, :]
        )
        read = jnp.sum(state * c_out[:, :, None, None, :], axis=-1) + d_skip[:, None] * x_val
        ssm_held = stored(state)
        gated = read * jax.nn.silu(gate_in.astype(jnp.float32))
        square_sum = jnp.sum(gated * gated, axis=(2, 3))
        stat_terms = square_sum[..., None] * group_mask
        totals = lax.psum(stat_terms, "row")
        mean_sq = lax.dynamic_index_in_dim(totals, group_index, 2, keepdims=False) / (
            group_heads * HDIM
        )
        normed = stored(gated * lax.rsqrt(mean_sq + EPS)[..., None, None] * gains)
        partial_out = jnp.einsum(
            "sbhp,hpd->sbd",
            lax.all_gather(normed, "beam", axis=1, tiled=True),
            w_out3,
            preferred_element_type=jnp.float32,
        )
        flat_rows = partial_out.reshape(sessions * width, partial_out.shape[2])
        outputs.append(
            lax.psum_scatter(flat_rows, "row", scatter_dimension=0, tiled=True).astype(jnp.bfloat16)
        )
    return (jnp.stack(outputs), ssm_held, conv_held, rim_held)


def solution(mesh):
    placed = (
        P(None, None, None, "beam"),
        P("beam", None, "row"),
        P("beam", None, "row"),
        P("beam", "row"),
        P(None, "row"),
        P(None, None, "row"),
        P("row"),
        P("row"),
        P("row"),
        P("row"),
        P("row", "beam"),
        P(None, "beam", "row", None, None),
        P(None, "beam", "row", None, None),
        P(None, "beam", None, None, "row"),
        P(),
    )
    return jax.shard_map(
        local,
        mesh=mesh,
        in_specs=placed,
        out_specs=(
            P(None, "row", "beam"),
            P(None, "beam", "row", None, None),
            P(None, "beam", "row", None, None),
            P(None, "beam", None, None, "row"),
        ),
        check_vma=False,
    )
```

profile of v0, /device:TPU:4, one launch (start us, length us, event | category | flops | bytes accessed | tf_op | source)
XLA Modules:
  0.0 760.4 jit_solution(5823953862466214772)
XLA Ops:
  7.2 4.8 copy.199
  12.1 1.1 convolution_bitcast_fusion.3
  13.2 0.8 copy.200
  14.0 1.1 convolution_bitcast_fusion.2
  15.1 0.8 copy.216
  16.0 1.1 convolution_bitcast_fusion.1
  17.0 0.8 copy.232
  17.9 1.1 convolution_bitcast_fusion
  19.0 0.8 copy.248
  19.9 2.3 copy.193
  24.1 22.1 %all-reduce.6 = (bf16[2,16,2,64]{3,1,2,0:T(8,128)(2,1)S(1)}, bf16[2,16,2,64]{3,1,2,0:T(8,128)(2,1)S(1)}, bf16[2,16,2,64]{3,1,2,0:T(8,128)(2,1)S(1)}, bf16[2,16,8...) all-reduce(f32[2,16,2,64]{3,1,2,0:T(8,128)S(1)} %fusion.30, ...), channel_id=1, replica_groups=mesh['beam'=8,'row'=32] {'beam'}, use_global_device_ids=true, to_apply=%region_22.23 | all-reduce | flops 17408 | bytes 104448 | tf_op jit(solution)/shard_map/psum | solution.py:82
  46.3 16.7 %all_gather.50 = bf16[2,16,3,2,64]{4,3,2,0,1:T(2,128)(2,1)S(1)} all-gather(bf16[2,2,3,2,64]{4,3,2,0,1:T(2,128)(2,1)S(1)} %copy.204), channel_id=1, replica_groups=mesh['beam'=8,'row'=32] {'beam'}, dimensions={1}, use_global_device_ids=true | all-gather | bytes 27648 | tf_op jit(solution)/shard_map/all_gather | solution.py:65
  63.3 12.8 %all_gather.54 = bf16[2,16,3,2,64]{4,3,2,0,1:T(2,128)(2,1)S(1)} all-gather(bf16[2,2,3,2,64]{4,3,2,0,1:T(2,128)(2,1)S(1)} %copy.220), channel_id=1, replica_groups=mesh['beam'=8,'row'=32] {'beam'}, dimensions={1}, use_global_device_ids=true | all-gather | bytes 27648 | tf_op jit(solution)/shard_map/all_gather | solution.py:65
  76.5 12.8 %all_gather.58 = bf16[2,16,3,2,64]{4,3,2,0,1:T(2,128)(2,1)S(1)} all-gather(bf16[2,2,3,2,64]{4,3,2,0,1:T(2,128)(2,1)S(1)} %copy.236), channel_id=1, replica_groups=mesh['beam'=8,'row'=32] {'beam'}, dimensions={1}, use_global_device_ids=true | all-gather | bytes 27648 | tf_op jit(solution)/shard_map/all_gather | solution.py:65
  89.6 12.8 %all_gather.62 = bf16[2,16,3,2,64]{4,3,2,0,1:T(2,128)(2,1)S(1)} all-gather(bf16[2,2,3,2,64]{4,3,2,0,1:T(2,128)(2,1)S(1)} %copy.252), channel_id=1, replica_groups=mesh['beam'=8,'row'=32] {'beam'}, dimensions={1}, use_global_device_ids=true | all-gather | bytes 27648 | tf_op jit(solution)/shard_map/all_gather | solution.py:65
  102.8 1.8 collective-permute-start
  104.6 12.8 %all_gather.49 = bf16[2,16,8,64,3]{3,2,4,0,1:T(8,128)(2,1)S(1)} all-gather(bf16[2,2,8,64,3]{3,2,4,0,1:T(8,128)(2,1)S(1)} %copy.196), channel_id=1, replica_groups=mesh['beam'=8,'row'=32] {'beam'}, dimensions={1}, use_global_device_ids=true | all-gather | bytes 110592 | tf_op jit(solution)/shard_map/all_gather | solution.py:64
  117.8 3.3 collective-permute-start.1
  121.4 1.3 collective-permute-done.1
  122.8 0.8 copy.343
  123.6 0.8 copy.342
  124.4 12.8 %all_gather.53 = bf16[2,16,8,64,3]{3,2,4,0,1:T(8,128)(2,1)S(1)} all-gather(bf16[2,2,8,64,3]{3,2,4,0,1:T(8,128)(2,1)S(1)} %copy.214), channel_id=1, replica_groups=mesh['beam'=8,'row'=32] {'beam'}, dimensions={1}, use_global_device_ids=true | all-gather | bytes 110592 | tf_op jit(solution)/shard_map/all_gather | solution.py:64
  137.6 0.8 copy.341
  138.4 12.8 %all_gather.57 = bf16[2,16,8,64,3]{3,2,4,0,1:T(8,128)(2,1)S(1)} all-gather(bf16[2,2,8,64,3]{3,2,4,0,1:T(8,128)(2,1)S(1)} %copy.230), channel_id=1, replica_groups=mesh['beam'=8,'row'=32] {'beam'}, dimensions={1}, use_global_device_ids=true | all-gather | bytes 110592 | tf_op jit(solution)/shard_map/all_gather | solution.py:64
  151.5 0.8 copy.340
  152.2 14.6 %all_gather.61 = bf16[2,16,8,64,3]{3,2,4,0,1:T(8,128)(2,1)S(1)} all-gather(bf16[2,2,8,64,3]{3,2,4,0,1:T(8,128)(2,1)S(1)} %copy.246), channel_id=1, replica_groups=mesh['beam'=8,'row'=32] {'beam'}, dimensions={1}, use_global_device_ids=true | all-gather | bytes 110592 | tf_op jit(solution)/shard_map/all_gather | solution.py:64
  167.4 39.3 %all-gather.5.cloned.1.call-done = bf16[2,16,8,64,256]{4,3,2,0,1:T(8,128)(2,1)} async-done(((bf16[2,2,8,64,256]{4,3,2,0,1:T(8,128)(2,1)}), bf16[2,16,8,64,256]{4,3,2,0,1:T(8,128)(2,1)}) %all-gather.5.cloned.1.call-update) | async-done | bytes 8388624 | tf_op jit(solution)/shard_map/all_gather | solution.py:63
  206.7 10.6 %multiply_reduce_fusion.3 = (f32[2,2,8,64]{1,3,2,0:T(8,128)S(1)}, bf16[2,2,8,64,256]{4,1,3,2,0:T(2,128)(2,1)S(1)}) fusion(f32[2,2,256]{2,1,0:T(2,128)S(1)} %get-tuple-element.64, f32[2,2,256]{2,1,0:T(2,128)S(1)} %get-tuple-element.65, f32[2,2,8,64]{1,3,2,0:T(8,128)S(1)} %copy.203, bf16[2,16,8,64,256]{4,3,2,0,1:T(8,128)(2,1)} %all-gather.5.cloned.1.call-done, ...), kind=kOutput, calls=%fused_computation.14 | convolution fusion | flops 20969536 | bytes 9461904 | tf_op jit(solution)/shard_map/sij,sjhpn->sihpn/dot_general | solution.py:70
  217.4 1.2 copy.210
  218.6 1.6 collective-permute-start.2
  220.3 2.0 collective-permute-done.2
  222.4 2.6 collective-permute-start.3
  225.0 1.9 collective-permute-done.3
  227.2 44.0 %all-gather.7.cloned.1.call-done = bf16[2,16,8,64,256]{4,3,2,0,1:T(8,128)(2,1)} async-done(((bf16[2,2,8,64,256]{4,3,2,0,1:T(8,128)(2,1)}), bf16[2,16,8,64,256]{4,3,2,0,1:T(8,128)(2,1)}) %all-gather.7.cloned.1.call-update) | async-done | bytes 8388624 | tf_op jit(solution)/shard_map/all_gather | solution.py:63
  271.2 10.6 %multiply_reduce_fusion.2 = (f32[2,2,8,64]{1,3,2,0:T(8,128)S(1)}, bf16[2,2,8,64,256]{4,1,3,2,0:T(2,128)(2,1)S(1)}) fusion(f32[2,2,256]{2,1,0:T(2,128)S(1)} %get-tuple-element.66, f32[2,2,256]{2,1,0:T(2,128)S(1)} %get-tuple-element.67, f32[2,2,8,64]{1,3,2,0:T(8,128)S(1)} %copy.219, bf16[2,16,8,64,256]{4,3,2,0,1:T(8,128)(2,1)} %all-gather.7.cloned.1.call-done, ...), kind=kOutput, calls=%fused_computation.12 | convolution fusion | flops 20969536 | bytes 9461904 | tf_op jit(solution)/shard_map/sij,sjhpn->sihpn/dot_general | solution.py:70
  281.8 1.2 copy.226
  283.1 1.8 collective-permute-start.4
  284.9 2.0 collective-permute-done.4
  287.0 2.6 collective-permute-start.5
  289.7 1.9 collective-permute-done.5
  291.8 43.8 %all-gather.9.cloned.1.call-done = bf16[2,16,8,64,256]{4,3,2,0,1:T(8,128)(2,1)} async-done(((bf16[2,2,8,64,256]{4,3,2,0,1:T(8,128)(2,1)}), bf16[2,16,8,64,256]{4,3,2,0,1:T(8,128)(2,1)}) %all-gather.9.cloned.1.call-update) | async-done | bytes 8388624 | tf_op jit(solution)/shard_map/all_gather | solution.py:63
  335.6 10.6 %multiply_reduce_fusion.1 = (f32[2,2,8,64]{1,3,2,0:T(8,128)S(1)}, bf16[2,2,8,64,256]{4,1,3,2,0:T(2,128)(2,1)S(1)}) fusion(f32[2,2,256]{2,1,0:T(2,128)S(1)} %get-tuple-element.68, f32[2,2,256]{2,1,0:T(2,128)S(1)} %get-tuple-element.69, f32[2,2,8,64]{1,3,2,0:T(8,128)S(1)} %copy.235, bf16[2,16,8,64,256]{4,3,2,0,1:T(8,128)(2,1)} %all-gather.9.cloned.1.call-done, ...), kind=kOutput, calls=%fused_computation.10 | convolution fusion | flops 20969536 | bytes 9461904 | tf_op jit(solution)/shard_map/sij,sjhpn->sihpn/dot_general | solution.py:70
  346.3 1.2 copy.242
  347.5 1.6 collective-permute-start.6
  349.2 2.0 collective-permute-done.6
  351.2 2.6 collective-permute-start.7
  354.0 0.6 copy.261
  354.6 0.6 dynamic-slice.4
  355.2 0.6 collective-permute-done.7
  356.2 0.6 copy.260
  357.5 42.7 %all-gather.11.cloned.1.call-done = bf16[2,16,8,64,256]{4,3,2,0,1:T(8,128)(2,1)} async-done(((bf16[2,2,8,64,256]{4,3,2,0,1:T(8,128)(2,1)}), bf16[2,16,8,64,256]{4,3,2,0,1:T(8,128)(2,1)}) %all-gather.11.cloned.1.call-update) | async-done | bytes 8388624 | tf_op jit(solution)/shard_map/all_gather | solution.py:63
  400.1 10.6 %fusion.172 = (bf16[2,2,8,64,256]{4,1,3,2,0:T(2,128)(2,1)S(1)}, f32[2,2,8,64]{1,3,2,0:T(8,128)S(1)}) fusion(f32[2,2,256]{2,1,0:T(2,128)S(1)} %get-tuple-element.70, f32[2,2,256]{2,1,0:T(2,128)S(1)} %get-tuple-element.71, f32[2,2,8,64]{1,3,2,0:T(8,128)S(1)} %copy.251, bf16[2,16,8,64,256]{4,3,2,0,1:T(8,128)(2,1)} %all-gather.11.cloned.1.call-done, ...), kind=kOutput, calls=%fused_computation.290 | convolution fusion | flops 20969536 | bytes 9461904 | tf_op jit(solution)/shard_map/sij,sjhpn->sihpn/dot_general | solution.py:70
  411.3 143.4 %all-reduce.5 = (f32[2,2,8]{1,0,2:T(2,128)S(1)}, f32[2,2,8]{1,0,2:T(2,128)S(1)}, f32[2,2,8]{1,0,2:T(2,128)S(1)}, f32[2,2,8]{1,0,2:T(2,128)S(1)}) all-reduce(f32[2,2,8]{1,0,2:T(2,128)S(1)} %get-tuple-element.105, f32[2,2,8]{1,0,2:T(2,128)S(1)} %get-tuple-element.104, ...), channel_id=1, replica_groups=mesh['beam'=8,'row'=32] {'row'}, use_global_device_ids=true, to_apply=%region_34.35 | all-reduce | flops 128 | bytes 1024 | tf_op jit(solution)/shard_map/psum | solution.py:132
  554.8 12.3 %all_gather.63 = bf16[2,16,8,64]{3,2,0,1:T(8,128)(2,1)S(1)} all-gather(bf16[2,2,8,64]{3,2,0,1:T(8,128)(2,1)S(1)} %copy.255), channel_id=1, replica_groups=mesh['beam'=8,'row'=32] {'beam'}, dimensions={1}, use_global_device_ids=true | all-gather | bytes 36864 | tf_op jit(solution)/shard_map/all_gather | solution.py:139
  567.4 12.7 %all_gather.59 = bf16[2,16,8,64]{3,2,0,1:T(8,128)(2,1)S(1)} all-gather(bf16[2,2,8,64]{3,2,0,1:T(8,128)(2,1)S(1)} %copy.239), channel_id=1, replica_groups=mesh['beam'=8,'row'=32] {'beam'}, dimensions={1}, use_global_device_ids=true | all-gather | bytes 36864 | tf_op jit(solution)/shard_map/all_gather | solution.py:139
  580.5 12.7 %all_gather.55 = bf16[2,16,8,64]{3,2,0,1:T(8,128)(2,1)S(1)} all-gather(bf16[2,2,8,64]{3,2,0,1:T(8,128)(2,1)S(1)} %copy.223), channel_id=1, replica_groups=mesh['beam'=8,'row'=32] {'beam'}, dimensions={1}, use_global_device_ids=true | all-gather | bytes 36864 | tf_op jit(solution)/shard_map/all_gather | solution.py:139
  593.6 12.7 %all_gather.51 = bf16[2,16,8,64]{3,2,0,1:T(8,128)(2,1)S(1)} all-gather(bf16[2,2,8,64]{3,2,0,1:T(8,128)(2,1)S(1)} %copy.207), channel_id=1, replica_groups=mesh['beam'=8,'row'=32] {'beam'}, dimensions={1}, use_global_device_ids=true | all-gather | bytes 36864 | tf_op jit(solution)/shard_map/all_gather | solution.py:139
  606.7 142.2 %all-reduce.8 = (bf16[32,1024]{1,0:T(8,128)(2,1)S(1)}, bf16[32,1024]{1,0:T(8,128)(2,1)S(1)}, bf16[32,1024]{1,0:T(8,128)(2,1)S(1)}, bf16[32,1024]{1,0:T(8,128)(2,1)S(1)}) all-reduce(f32[32,1024]{1,0:T(8,128)S(1)} %convolution_bitcast_fusion.4, ...), channel_id=9, replica_groups=mesh['beam'=8,'row'=32] {'row'}, use_global_device_ids=true, to_apply=%region_35.36.clone | all-reduce | flops 131072 | bytes 786432
  748.9 0.7 fusion.112
  749.6 0.7 fusion.113
  750.3 0.7 fusion.114
  750.9 0.7 fusion.115
  751.6 1.2 copy.259
  752.8 0.6 pad_maximum_fusion.4
  (166 shorter events, 9.8 us)
Async XLA Ops:
  7.2 559.9 %copy-start = (bf16[512,1024]{1,0:T(8,128)(2,1)S(1)}, bf16[512,1024]{1,0:T(8,128)(2,1)}, u32[]{:S(2)}) copy-start(bf16[512,1024]{1,0:T(8,128)(2,1)} %param.25) | copy-start | bytes 3145732
  7.2 4.9 copy-start.2
  7.2 115.6 %reduce-scatter.5.cloned.1.call-start = ((), (), s32[]{:S(2)}) async-start(), calls=%async_computation.5 | async-start | bytes 294912 | tf_op jit(solution)/shard_map/reduce_scatter | solution.py:88
  14.0 109.6 %reduce-scatter.7.cloned.1.call-start = ((), (), s32[]{:S(2)}) async-start(), calls=%async_computation.7 | async-start | bytes 294912 | tf_op jit(solution)/shard_map/reduce_scatter | solution.py:88
  15.9 121.6 %reduce-scatter.9.cloned.1.call-start = ((), (), s32[]{:S(2)}) async-start(), calls=%async_computation.9 | async-start | bytes 294912 | tf_op jit(solution)/shard_map/reduce_scatter | solution.py:88
  17.9 133.6 %reduce-scatter.11.cloned.1.call-start = ((), (), s32[]{:S(2)}) async-start(), calls=%async_computation.11 | async-start | bytes 294912 | tf_op jit(solution)/shard_map/reduce_scatter | solution.py:88
  19.0 3.3 copy-start.5
  19.0 3.4 copy-start.11
  19.0 4.1 copy-start.1
  19.9 26.4 %copy-start.6 = (bf16[2,2,3,2,64]{4,3,2,1,0:T(2,128)(2,1)S(1)}, bf16[2,2,3,2,64]{4,3,2,1,0:T(2,128)(2,1)}, u32[]{:S(2)}) copy-start(bf16[2,2,3,2,64]{4,3,2,1,0:T(2,128)(2,1)} %param.28) | copy-start | bytes 9220
  19.9 186.9 %all-gather.5.cloned.1.call-start = ((), (), s32[]{:S(2)}) async-start(), calls=%async_computation.4 | async-start | bytes 9437184 | tf_op jit(solution)/shard_map/all_gather | solution.py:63
  22.2 40.7 %copy-start.7 = (s32[4,2,16]{2,1,0:T(2,128)S(1)}, s32[4,2,16]{2,1,0:T(2,128)}, u32[]{:S(2)}) copy-start(s32[4,2,16]{2,1,0:T(2,128)} %param.29) | copy-start | bytes 1540
  22.2 82.3 %copy-start.4 = (bf16[2,2,8,64,3]{3,2,4,1,0:T(8,128)(2,1)S(1)}, bf16[2,2,8,64,3]{3,2,4,1,0:T(8,128)(2,1)}, u32[]{:S(2)}) copy-start(bf16[2,2,8,64,3]{3,2,4,1,0:T(8,128)(2,1)} %param.27) | copy-start | bytes 36868
  22.2 95.1 %copy-start.12 = (f32[8]{0:T(128)S(1)}, f32[8]{0:T(128)}, u32[]{:S(2)}) copy-start(f32[8]{0:T(128)} %param.22) | copy-start | bytes 100
  22.2 95.3 %copy-start.9 = (f32[8]{0:T(128)S(1)}, f32[8]{0:T(128)}, u32[]{:S(2)}) copy-start(f32[8]{0:T(128)} %param.21) | copy-start | bytes 100
  22.2 95.5 %copy-start.3 = (bf16[4,512]{1,0:T(4,128)(2,1)S(1)}, bf16[4,512]{1,0:T(4,128)(2,1)}, u32[]{:S(2)}) copy-start(bf16[4,512]{1,0:T(4,128)(2,1)} %param.19) | copy-start | bytes 12292
  22.3 248.9 %all-gather.7.cloned.1.call-start = ((), (), s32[]{:S(2)}) async-start(), calls=%async_computation.6 | async-start | bytes 9437184 | tf_op jit(solution)/shard_map/all_gather | solution.py:63
  102.8 15.0 %collective-permute-start = (bf16[2,2,2,64]{3,1,2,0:T(2,128)(2,1)S(1)}, bf16[2,2,2,64]{3,1,2,0:T(2,128)(2,1)S(1)}, u32[]{:S(2)}, u32[]{:S(2)}) collective-permute-start(bf16[2,2,2,64]{3,1,2,0:T(2,128)(2,1)S(1)} %get-tuple-element.101), channel_id=1, source_target_pairs={{0,1},{1,0},{2,3},{3,2},{4,5},{5,4},{6,7},{7,6},{8,9},{9,8},{10,11... | collective-permute-start | bytes 3080 | tf_op jit(solution)/shard_map/ppermute | solution.py:13
  117.8 4.9 collective-permute-start.1
  218.6 117.1 %all-gather.9.cloned.1.call-start = ((), (), s32[]{:S(2)}) async-start(), calls=%async_computation.8 | async-start | bytes 9437184 | tf_op jit(solution)/shard_map/all_gather | solution.py:63
  218.6 3.7 collective-permute-start.2
  222.4 4.5 collective-permute-start.3
  283.0 117.1 %all-gather.11.cloned.1.call-start = ((), (), s32[]{:S(2)}) async-start(), calls=%async_computation.10 | async-start | bytes 9437184 | tf_op jit(solution)/shard_map/all_gather | solution.py:63
  283.1 3.8 collective-permute-start.4
  287.0 4.5 collective-permute-start.5
  346.3 7.6 %copy-start.8 = (f32[512]{0:T(512)S(1)}, f32[512]{0:T(512)}, u32[]{:S(2)}) copy-start(f32[512]{0:T(512)} %param.24) | copy-start | bytes 6148
  346.3 8.3 %copy-start.13 = (u32[256]{0:T(256)S(1)}, u32[256]{0:T(256)}, u32[]{:S(2)}) copy-start(u32[256]{0:T(256)} %constant.86) | copy-start | bytes 3076
  347.5 3.7 collective-permute-start.6
  351.2 4.5 collective-permute-start.7
  400.1 10.8 %copy-start.10 = (f32[8]{0:T(128)S(1)}, f32[8]{0:T(128)}, u32[]{:S(2)}) copy-start(f32[8]{0:T(128)} %param.23) | copy-start | bytes 100
Sparse Core Ops, SparseCore 0:
  14.1 30.9 reduce-scatter.4
  47.8 31.9 reduce-scatter.6
  82.3 31.9 reduce-scatter.8
  116.8 32.1 reduce-scatter.10
  151.3 55.4 all-gather.4
  218.7 52.4 all-gather.6
  283.1 52.4 all-gather.8
  347.6 52.4 all-gather.10
where the time goes:
time: 769 us; the launch traced here: 760 us
  blocking collectives  466 us (61%)
  waiting for transfers between devices  182 us (24%)
  matrix products  51.5 us (7%)
  local copies, waits for them, and re-layouts  25.6 us (3%)
  starting transfers between devices  18.3 us (2%)
  between operations  15 us (2%)
    all_gather x4, waiting for transfers between devices, local(): lax.all_gather(ssm_held, 'beam', axis=1, tiled=True)  170 us
    psum x1, blocking collectives, local(): totals = lax.psum(stat_terms, 'row')  143 us
    unnamed x1, blocking collectives  142 us
    all_gather x4, blocking collectives, local(): lax.all_gather(rim_held, 'beam', axis=1, tiled=True)  55.1 us
    all_gather x4, blocking collectives, local(): lax.all_gather(conv_held, 'beam', axis=1, tiled=True)  52.9 us
    all_gather x4, blocking collectives, local(): lax.all_gather(normed, 'beam', axis=1, tiled=True)  50.6 us
    dot_general x4, matrix products, local(): jnp.einsum('sij,sjhpn->sihpn', choose, pieces[0], preferred_element_type=...  42.5 us
    psum x1, blocking collectives, local(): bc_sum, dt_sum = lax.psum((bc_part, dt_part), 'beam')  22.1 us
  transfers between devices with their start and end apart: 16, of which 11 were waited for; matrix products, arithmetic and copies ran while one was open for 3% of the time, Pallas kernels for 0%

commit v1 on v0

--- a/solution.py
+++ b/solution.py
@@ -136,7 +136,9 @@
         normed = stored(gated * lax.rsqrt(mean_sq + EPS)[..., None, None] * gains)
         partial_out = jnp.einsum(
             "sbhp,hpd->sbd",
-            lax.all_gather(normed, "beam", axis=1, tiled=True),
+            jnp.concatenate(
+                lax.all_to_all(jnp.stack([normed] * lax.axis_size("beam")), "beam", 0, 0), axis=1
+            ),
             w_out3,
             preferred_element_type=jnp.float32,
         )

time: 769 us -> 752 us (0.978)
  blocking collectives: 466 us -> 416 us
  starting transfers between devices: 18.3 us -> 39.8 us
    all_gather x4 -> x0, blocking collectives: 50.6 us -> none  [local(): lax.all_gather(normed, 'beam', axis=1, tiled=True)]
    all_to_all x0 -> x4, starting transfers between devices: none -> 21.5 us  [local(): lax.all_to_all(jnp.stack([normed] * lax.axis_size('beam')), 'beam', 0, 0)]
  transfers between devices with their start and end apart: 16 -> 20, of which waited for: 11 -> 14; matrix products, arithmetic and copies ran while one was open for 3% -> 3% of each run, Pallas kernels for 0% -> 0%
where the time goes in v1:
time: 752 us; the launch traced here: 743 us
  blocking collectives  416 us (55%)
  waiting for transfers between devices  189 us (25%)
  matrix products  51.5 us (7%)
  starting transfers between devices  39.8 us (5%)
  local copies, waits for them, and re-layouts  29.5 us (4%)
  between operations  15.2 us (2%)
    all_gather x4, waiting for transfers between devices, local(): lax.all_gather(ssm_held, 'beam', axis=1, tiled=True)  170 us
    psum x1, blocking collectives, local(): totals = lax.psum(stat_terms, 'row')  143 us
    unnamed x1, blocking collectives  142 us
    all_gather x4, blocking collectives, local(): lax.all_gather(rim_held, 'beam', axis=1, tiled=True)  55.1 us
    all_gather x4, blocking collectives, local(): lax.all_gather(conv_held, 'beam', axis=1, tiled=True)  52.9 us
    dot_general x4, matrix products, local(): jnp.einsum('sij,sjhpn->sihpn', choose, pieces[0], preferred_element_type=...  42.5 us
    psum x1, blocking collectives, local(): bc_sum, dt_sum = lax.psum((bc_part, dt_part), 'beam')  22.1 us
    all_to_all x4, starting transfers between devices, local(): lax.all_to_all(jnp.stack([normed] * lax.axis_size('beam')), 'beam', 0, 0)  21.5 us
  transfers between devices with their start and end apart: 20, of which 14 were waited for; matrix products, arithmetic and copies ran while one was open for 3% of the time, Pallas kernels for 0%

profile of v1, /device:TPU:4, one launch (start us, length us, event | category | flops | bytes accessed | tf_op | source)
XLA Modules:
  0.0 742.6 jit_solution(16865093424822446280)
XLA Ops:
  7.2 4.8 copy.191
  12.1 1.1 convolution_bitcast_fusion.3
  13.2 0.8 copy.192
  14.0 1.1 convolution_bitcast_fusion.2
  15.1 0.8 copy.207
  16.0 1.1 convolution_bitcast_fusion.1
  17.1 0.8 copy.222
  18.0 1.1 convolution_bitcast_fusion
  19.1 0.8 copy.237
  19.9 2.3 copy.185
  24.1 22.1 %all-reduce.6 = (bf16[2,16,2,64]{3,1,2,0:T(8,128)(2,1)S(1)}, bf16[2,16,2,64]{3,1,2,0:T(8,128)(2,1)S(1)}, bf16[2,16,2,64]{3,1,2,0:T(8,128)(2,1)S(1)}, bf16[2,16,8...) all-reduce(f32[2,16,2,64]{3,1,2,0:T(8,128)S(1)} %fusion.30, ...), channel_id=1, replica_groups=mesh['beam'=8,'row'=32] {'beam'}, use_global_device_ids=true, to_apply=%region_22.23 | all-reduce | flops 17408 | bytes 104448 | tf_op jit(solution)/shard_map/psum | solution.py:82
  46.3 16.7 %all_gather.38 = bf16[2,16,3,2,64]{4,3,2,0,1:T(2,128)(2,1)S(1)} all-gather(bf16[2,2,3,2,64]{4,3,2,0,1:T(2,128)(2,1)S(1)} %copy.196), channel_id=1, replica_groups=mesh['beam'=8,'row'=32] {'beam'}, dimensions={1}, use_global_device_ids=true | all-gather | bytes 27648 | tf_op jit(solution)/shard_map/all_gather | solution.py:65
  63.3 12.8 %all_gather.41 = bf16[2,16,3,2,64]{4,3,2,0,1:T(2,128)(2,1)S(1)} all-gather(bf16[2,2,3,2,64]{4,3,2,0,1:T(2,128)(2,1)S(1)} %copy.211), channel_id=1, replica_groups=mesh['beam'=8,'row'=32] {'beam'}, dimensions={1}, use_global_device_ids=true | all-gather | bytes 27648 | tf_op jit(solution)/shard_map/all_gather | solution.py:65
  76.5 12.8 %all_gather.44 = bf16[2,16,3,2,64]{4,3,2,0,1:T(2,128)(2,1)S(1)} all-gather(bf16[2,2,3,2,64]{4,3,2,0,1:T(2,128)(2,1)S(1)} %copy.226), channel_id=1, replica_groups=mesh['beam'=8,'row'=32] {'beam'}, dimensions={1}, use_global_device_ids=true | all-gather | bytes 27648 | tf_op jit(solution)/shard_map/all_gather | solution.py:65
  89.6 12.8 %all_gather.47 = bf16[2,16,3,2,64]{4,3,2,0,1:T(2,128)(2,1)S(1)} all-gather(bf16[2,2,3,2,64]{4,3,2,0,1:T(2,128)(2,1)S(1)} %copy.241), channel_id=1, replica_groups=mesh['beam'=8,'row'=32] {'beam'}, dimensions={1}, use_global_device_ids=true | all-gather | bytes 27648 | tf_op jit(solution)/shard_map/all_gather | solution.py:65
  102.8 1.8 collective-permute-start
  104.6 12.8 %all_gather.37 = bf16[2,16,8,64,3]{3,2,4,0,1:T(8,128)(2,1)S(1)} all-gather(bf16[2,2,8,64,3]{3,2,4,0,1:T(8,128)(2,1)S(1)} %copy.188), channel_id=1, replica_groups=mesh['beam'=8,'row'=32] {'beam'}, dimensions={1}, use_global_device_ids=true | all-gather | bytes 110592 | tf_op jit(solution)/shard_map/all_gather | solution.py:64
  117.8 3.3 collective-permute-start.1
  121.5 1.3 collective-permute-done.1
  122.8 0.8 copy.323
  123.6 0.8 copy.322
  124.4 12.8 %all_gather.40 = bf16[2,16,8,64,3]{3,2,4,0,1:T(8,128)(2,1)S(1)} all-gather(bf16[2,2,8,64,3]{3,2,4,0,1:T(8,128)(2,1)S(1)} %copy.205), channel_id=1, replica_groups=mesh['beam'=8,'row'=32] {'beam'}, dimensions={1}, use_global_device_ids=true | all-gather | bytes 110592 | tf_op jit(solution)/shard_map/all_gather | solution.py:64
  137.6 0.8 copy.321
  138.4 12.8 %all_gather.43 = bf16[2,16,8,64,3]{3,2,4,0,1:T(8,128)(2,1)S(1)} all-gather(bf16[2,2,8,64,3]{3,2,4,0,1:T(8,128)(2,1)S(1)} %copy.220), channel_id=1, replica_groups=mesh['beam'=8,'row'=32] {'beam'}, dimensions={1}, use_global_device_ids=true | all-gather | bytes 110592 | tf_op jit(solution)/shard_map/all_gather | solution.py:64
  151.5 0.8 copy.320
  152.3 14.5 %all_gather.46 = bf16[2,16,8,64,3]{3,2,4,0,1:T(8,128)(2,1)S(1)} all-gather(bf16[2,2,8,64,3]{3,2,4,0,1:T(8,128)(2,1)S(1)} %copy.235), channel_id=1, replica_groups=mesh['beam'=8,'row'=32] {'beam'}, dimensions={1}, use_global_device_ids=true | all-gather | bytes 110592 | tf_op jit(solution)/shard_map/all_gather | solution.py:64
  167.4 39.3 %all-gather.5.cloned.1.call-done = bf16[2,16,8,64,256]{4,3,2,0,1:T(8,128)(2,1)} async-done(((bf16[2,2,8,64,256]{4,3,2,0,1:T(8,128)(2,1)}), bf16[2,16,8,64,256]{4,3,2,0,1:T(8,128)(2,1)}) %all-gather.5.cloned.1.call-update) | async-done | bytes 8388624 | tf_op jit(solution)/shard_map/all_gather | solution.py:63
  206.7 10.6 %multiply_reduce_fusion.3 = (f32[2,2,8,64]{1,3,2,0:T(8,128)S(1)}, bf16[2,2,8,64,256]{4,1,3,2,0:T(2,128)(2,1)S(1)}) fusion(f32[2,2,256]{2,1,0:T(2,128)S(1)} %get-tuple-element.64, f32[2,2,256]{2,1,0:T(2,128)S(1)} %get-tuple-element.65, f32[2,2,8,64]{1,3,2,0:T(8,128)S(1)} %copy.195, bf16[2,16,8,64,256]{4,3,2,0,1:T(8,128)(2,1)} %all-gather.5.cloned.1.call-done, ...), kind=kOutput, calls=%fused_computation.14 | convolution fusion | flops 20969536 | bytes 9461904 | tf_op jit(solution)/shard_map/sij,sjhpn->sihpn/dot_general | solution.py:70
  217.3 1.2 copy.201
  218.6 1.7 collective-permute-start.2
  220.3 2.0 collective-permute-done.2
  222.3 2.6 collective-permute-start.3
  225.0 1.9 collective-permute-done.3
  227.2 44.0 %all-gather.7.cloned.1.call-done = bf16[2,16,8,64,256]{4,3,2,0,1:T(8,128)(2,1)} async-done(((bf16[2,2,8,64,256]{4,3,2,0,1:T(8,128)(2,1)}), bf16[2,16,8,64,256]{4,3,2,0,1:T(8,128)(2,1)}) %all-gather.7.cloned.1.call-update) | async-done | bytes 8388624 | tf_op jit(solution)/shard_map/all_gather | solution.py:63
  271.1 10.6 %multiply_reduce_fusion.2 = (f32[2,2,8,64]{1,3,2,0:T(8,128)S(1)}, bf16[2,2,8,64,256]{4,1,3,2,0:T(2,128)(2,1)S(1)}) fusion(f32[2,2,256]{2,1,0:T(2,128)S(1)} %get-tuple-element.66, f32[2,2,256]{2,1,0:T(2,128)S(1)} %get-tuple-element.67, f32[2,2,8,64]{1,3,2,0:T(8,128)S(1)} %copy.210, bf16[2,16,8,64,256]{4,3,2,0,1:T(8,128)(2,1)} %all-gather.7.cloned.1.call-done, ...), kind=kOutput, calls=%fused_computation.12 | convolution fusion | flops 20969536 | bytes 9461904 | tf_op jit(solution)/shard_map/sij,sjhpn->sihpn/dot_general | solution.py:70
  281.8 1.2 copy.216
  283.0 1.8 collective-permute-start.4
  284.8 2.0 collective-permute-done.4
  287.0 2.6 collective-permute-start.5
  289.6 1.9 collective-permute-done.5
  291.8 43.8 %all-gather.9.cloned.1.call-done = bf16[2,16,8,64,256]{4,3,2,0,1:T(8,128)(2,1)} async-done(((bf16[2,2,8,64,256]{4,3,2,0,1:T(8,128)(2,1)}), bf16[2,16,8,64,256]{4,3,2,0,1:T(8,128)(2,1)}) %all-gather.9.cloned.1.call-update) | async-done | bytes 8388624 | tf_op jit(solution)/shard_map/all_gather | solution.py:63
  335.6 10.6 %multiply_reduce_fusion.1 = (f32[2,2,8,64]{1,3,2,0:T(8,128)S(1)}, bf16[2,2,8,64,256]{4,1,3,2,0:T(2,128)(2,1)S(1)}) fusion(f32[2,2,256]{2,1,0:T(2,128)S(1)} %get-tuple-element.68, f32[2,2,256]{2,1,0:T(2,128)S(1)} %get-tuple-element.69, f32[2,2,8,64]{1,3,2,0:T(8,128)S(1)} %copy.225, bf16[2,16,8,64,256]{4,3,2,0,1:T(8,128)(2,1)} %all-gather.9.cloned.1.call-done, ...), kind=kOutput, calls=%fused_computation.10 | convolution fusion | flops 20969536 | bytes 9461904 | tf_op jit(solution)/shard_map/sij,sjhpn->sihpn/dot_general | solution.py:70
  346.3 1.2 copy.231
  347.5 1.6 collective-permute-start.6
  349.1 2.0 collective-permute-done.6
  351.2 2.6 collective-permute-start.7
  357.4 42.7 %all-gather.11.cloned.1.call-done = bf16[2,16,8,64,256]{4,3,2,0,1:T(8,128)(2,1)} async-done(((bf16[2,2,8,64,256]{4,3,2,0,1:T(8,128)(2,1)}), bf16[2,16,8,64,256]{4,3,2,0,1:T(8,128)(2,1)}) %all-gather.11.cloned.1.call-update) | async-done | bytes 8388624 | tf_op jit(solution)/shard_map/all_gather | solution.py:63
  400.1 10.6 %fusion.168 = (bf16[2,2,8,64,256]{4,1,3,2,0:T(2,128)(2,1)S(1)}, f32[2,2,8,64]{1,3,2,0:T(8,128)S(1)}) fusion(f32[2,2,256]{2,1,0:T(2,128)S(1)} %get-tuple-element.70, f32[2,2,256]{2,1,0:T(2,128)S(1)} %get-tuple-element.71, f32[2,2,8,64]{1,3,2,0:T(8,128)S(1)} %copy.240, bf16[2,16,8,64,256]{4,3,2,0,1:T(8,128)(2,1)} %all-gather.11.cloned.1.call-done, ...), kind=kOutput, calls=%fused_computation.286 | convolution fusion | flops 20969536 | bytes 9461904 | tf_op jit(solution)/shard_map/sij,sjhpn->sihpn/dot_general | solution.py:70
  411.2 143.4 %all-reduce.5 = (f32[2,2,8]{1,0,2:T(2,128)S(1)}, f32[2,2,8]{1,0,2:T(2,128)S(1)}, f32[2,2,8]{1,0,2:T(2,128)S(1)}, f32[2,2,8]{1,0,2:T(2,128)S(1)}) all-reduce(f32[2,2,8]{1,0,2:T(2,128)S(1)} %get-tuple-element.105, f32[2,2,8]{1,0,2:T(2,128)S(1)} %get-tuple-element.104, ...), channel_id=1, replica_groups=mesh['beam'=8,'row'=32] {'row'}, use_global_device_ids=true, to_apply=%region_34.35 | all-reduce | flops 128 | bytes 1024 | tf_op jit(solution)/shard_map/psum | solution.py:132
  554.8 0.7 reshape.199
  555.5 4.9 all-to-all-start.3
  560.6 0.7 reshape.201
  561.3 0.7 reshape.203
  562.0 0.7 reshape.205
  562.7 1.2 copy.247
  563.9 5.2 all-to-all-start.2
  569.3 2.8 all-to-all-done.2
  572.1 5.7 all-to-all-start.1
  578.7 2.1 all-to-all-done.1
  580.8 5.7 all-to-all-start
  587.1 2.5 all-to-all-done
  590.1 142.2 %all-reduce.8 = (bf16[32,1024]{1,0:T(8,128)(2,1)S(1)}, bf16[32,1024]{1,0:T(8,128)(2,1)S(1)}, bf16[32,1024]{1,0:T(8,128)(2,1)S(1)}, bf16[32,1024]{1,0:T(8,128)(2,1)S(1)}) all-reduce(f32[32,1024]{1,0:T(8,128)S(1)} %convolution_bitcast_fusion.4, ...), channel_id=9, replica_groups=mesh['beam'=8,'row'=32] {'row'}, use_global_device_ids=true, to_apply=%region_35.36.clone | all-reduce | flops 131072 | bytes 786432
  732.3 0.7 fusion.108
  732.9 0.7 fusion.109
  (186 shorter events, 15.1 us)
Async XLA Ops:
  7.2 570.9 %copy-start = (bf16[512,1024]{1,0:T(8,128)(2,1)S(1)}, bf16[512,1024]{1,0:T(8,128)(2,1)}, u32[]{:S(2)}) copy-start(bf16[512,1024]{1,0:T(8,128)(2,1)} %param.25) | copy-start | bytes 3145732
  7.2 4.9 copy-start.2
  7.2 115.6 %reduce-scatter.5.cloned.1.call-start = ((), (), s32[]{:S(2)}) async-start(), calls=%async_computation.9 | async-start | bytes 294912 | tf_op jit(solution)/shard_map/reduce_scatter | solution.py:88
  14.0 109.6 %reduce-scatter.7.cloned.1.call-start = ((), (), s32[]{:S(2)}) async-start(), calls=%async_computation.11 | async-start | bytes 294912 | tf_op jit(solution)/shard_map/reduce_scatter | solution.py:88
  15.9 121.6 %reduce-scatter.9.cloned.1.call-start = ((), (), s32[]{:S(2)}) async-start(), calls=%async_computation.13 | async-start | bytes 294912 | tf_op jit(solution)/shard_map/reduce_scatter | solution.py:88
  17.9 133.6 %reduce-scatter.11.cloned.1.call-start = ((), (), s32[]{:S(2)}) async-start(), calls=%async_computation.15 | async-start | bytes 294912 | tf_op jit(solution)/shard_map/reduce_scatter | solution.py:88
  19.0 3.3 copy-start.5
  19.0 3.3 copy-start.11
  19.0 4.1 copy-start.1
  19.9 26.4 %copy-start.6 = (bf16[2,2,3,2,64]{4,3,2,1,0:T(2,128)(2,1)S(1)}, bf16[2,2,3,2,64]{4,3,2,1,0:T(2,128)(2,1)}, u32[]{:S(2)}) copy-start(bf16[2,2,3,2,64]{4,3,2,1,0:T(2,128)(2,1)} %param.28) | copy-start | bytes 9220
  19.9 186.8 %all-gather.5.cloned.1.call-start = ((), (), s32[]{:S(2)}) async-start(), calls=%async_computation.8 | async-start | bytes 9437184 | tf_op jit(solution)/shard_map/all_gather | solution.py:63
  22.2 40.7 %copy-start.7 = (s32[4,2,16]{2,1,0:T(2,128)S(1)}, s32[4,2,16]{2,1,0:T(2,128)}, u32[]{:S(2)}) copy-start(s32[4,2,16]{2,1,0:T(2,128)} %param.29) | copy-start | bytes 1540
  22.2 82.3 %copy-start.4 = (bf16[2,2,8,64,3]{3,2,4,1,0:T(8,128)(2,1)S(1)}, bf16[2,2,8,64,3]{3,2,4,1,0:T(8,128)(2,1)}, u32[]{:S(2)}) copy-start(bf16[2,2,8,64,3]{3,2,4,1,0:T(8,128)(2,1)} %param.27) | copy-start | bytes 36868
  22.2 95.1 %copy-start.12 = (f32[8]{0:T(128)S(1)}, f32[8]{0:T(128)}, u32[]{:S(2)}) copy-start(f32[8]{0:T(128)} %param.22) | copy-start | bytes 100
  22.2 95.3 %copy-start.9 = (f32[8]{0:T(128)S(1)}, f32[8]{0:T(128)}, u32[]{:S(2)}) copy-start(f32[8]{0:T(128)} %param.21) | copy-start | bytes 100
  22.3 95.5 %copy-start.3 = (bf16[4,512]{1,0:T(4,128)(2,1)S(1)}, bf16[4,512]{1,0:T(4,128)(2,1)}, u32[]{:S(2)}) copy-start(bf16[4,512]{1,0:T(4,128)(2,1)} %param.19) | copy-start | bytes 12292
  22.3 248.9 %all-gather.7.cloned.1.call-start = ((), (), s32[]{:S(2)}) async-start(), calls=%async_computation.10 | async-start | bytes 9437184 | tf_op jit(solution)/shard_map/all_gather | solution.py:63
  102.8 15.0 %collective-permute-start = (bf16[2,2,2,64]{3,1,2,0:T(2,128)(2,1)S(1)}, bf16[2,2,2,64]{3,1,2,0:T(2,128)(2,1)S(1)}, u32[]{:S(2)}, u32[]{:S(2)}) collective-permute-start(bf16[2,2,2,64]{3,1,2,0:T(2,128)(2,1)S(1)} %get-tuple-element.101), channel_id=1, source_target_pairs={{0,1},{1,0},{2,3},{3,2},{4,5},{5,4},{6,7},{7,6},{8,9},{9,8},{10,11... | collective-permute-start | bytes 3080 | tf_op jit(solution)/shard_map/ppermute | solution.py:13
  117.8 4.9 collective-permute-start.1
  218.5 117.1 %all-gather.9.cloned.1.call-start = ((), (), s32[]{:S(2)}) async-start(), calls=%async_computation.12 | async-start | bytes 9437184 | tf_op jit(solution)/shard_map/all_gather | solution.py:63
  218.6 3.7 collective-permute-start.2
  222.3 4.5 collective-permute-start.3
  283.0 117.1 %all-gather.11.cloned.1.call-start = ((), (), s32[]{:S(2)}) async-start(), calls=%async_computation.14 | async-start | bytes 9437184 | tf_op jit(solution)/shard_map/all_gather | solution.py:63
  283.0 3.8 collective-permute-start.4
  287.0 4.5 collective-permute-start.5
  346.2 7.6 %copy-start.8 = (f32[512]{0:T(512)S(1)}, f32[512]{0:T(512)}, u32[]{:S(2)}) copy-start(f32[512]{0:T(512)} %param.24) | copy-start | bytes 6148
  346.2 8.3 %copy-start.13 = (u32[256]{0:T(256)S(1)}, u32[256]{0:T(256)}, u32[]{:S(2)}) copy-start(u32[256]{0:T(256)} %constant.86) | copy-start | bytes 3076
  347.5 3.7 collective-permute-start.6
  351.2 4.5 collective-permute-start.7
  400.1 10.8 %copy-start.10 = (f32[8]{0:T(128)S(1)}, f32[8]{0:T(128)}, u32[]{:S(2)}) copy-start(f32[8]{0:T(128)} %param.23) | copy-start | bytes 100
  555.5 8.4 %all-to-all-start.3 = ((bf16[8,2,1024]{2,1,0:T(2,128)(2,1)}), bf16[8,2,1024]{2,1,0:T(2,128)(2,1)S(1)}, u32[]{:S(2)}, u32[]{:S(2)}) async-start(bf16[8,2,1024]{2,1,0:T(2,128)(2,1)} %reshape.199), calls=%async_computation.7 | async-start | bytes 65536 | tf_op jit(solution)/shard_map/all_to_all | solution.py:140
  563.9 8.2 %all-to-all-start.2 = ((bf16[8,2,1024]{2,1,0:T(2,128)(2,1)}), bf16[8,2,1024]{2,1,0:T(2,128)(2,1)S(1)}, u32[]{:S(2)}, u32[]{:S(2)}) async-start(bf16[8,2,1024]{2,1,0:T(2,128)(2,1)} %reshape.201), calls=%async_computation.5 | async-start | bytes 65536 | tf_op jit(solution)/shard_map/all_to_all | solution.py:140
  572.1 8.7 %all-to-all-start.1 = ((bf16[8,2,1024]{2,1,0:T(2,128)(2,1)}), bf16[8,2,1024]{2,1,0:T(2,128)(2,1)S(1)}, u32[]{:S(2)}, u32[]{:S(2)}) async-start(bf16[8,2,1024]{2,1,0:T(2,128)(2,1)} %reshape.203), calls=%async_computation.3 | async-start | bytes 65536 | tf_op jit(solution)/shard_map/all_to_all | solution.py:140
  580.8 8.7 %all-to-all-start = ((bf16[8,2,1024]{2,1,0:T(2,128)(2,1)}), bf16[8,2,1024]{2,1,0:T(2,128)(2,1)S(1)}, u32[]{:S(2)}, u32[]{:S(2)}) async-start(bf16[8,2,1024]{2,1,0:T(2,128)(2,1)} %reshape.205), calls=%async_computation.1 | async-start | bytes 65536 | tf_op jit(solution)/shard_map/all_to_all | solution.py:140
Sparse Core Ops, SparseCore 0:
  14.1 30.9 reduce-scatter.4
  47.8 31.8 reduce-scatter.6
  82.2 31.9 reduce-scatter.8
  116.8 32.1 reduce-scatter.10
  151.3 55.3 all-gather.4
  218.7 52.4 all-gather.6
  283.1 52.4 all-gather.8
  347.6 52.4 all-gather.10
